TPU v7x, 512 devices: a whole 4x8x8 slice. The times are simulated.
512 devices in a mesh: row: 16 (over z, core), col: 32 (over x, y).
Axes of the slice: x: 4, y: 8, z: 8, core: 2. Of those that a mesh axis runs over, the one named last changes fastest.
Arguments:
- panel: bfloat16 [64, 1024, 256], P('row', 'col'), may hold values from -6 to 6
- inverse_factor: bfloat16 [1024, 1024], P('row', 'col'), as said below
- ranks: int32 [64], replicated, may hold values from 32 to 256
Outputs:
- solved: bfloat16 [64, 1024, 256], P('row', 'col')
- core_blocks: bfloat16 [64, 64, 256, 256], P('row', 'col')
Inputs may be any that keep to these rules, and one draw needn't show every extreme that they name: inverse_factor is lower triangular with a diagonal between 0.5 and 3.
All inputs are finite; a program needn't handle non-finite values.
Results may differ from a plain program's by a relative error of at most 0.017.
Values may be sent and summed in bfloat16 or wider, within the bound.
No kernel may reach another device: no remote copies, remote signals or barrier semaphores. Data moves between devices by JAX's collectives and lax.ppermute only.
A program may use at most 64 MiB of HBM per device.

v0:
```python
import jax
import jax.numpy as jnp
from jax import lax
from jax.sharding import Mesh
from jax.sharding import PartitionSpec as P

ROW = ("z", "core")
COL = ("x", "y")
ALL = ROW + COL


def size_of(axes):
    axes = axes if isinstance(axes, tuple) else (axes,)
    count = 1
    for axis in axes:
        count *= lax.axis_size(axis)
    return count


def sent_to_all(value, axes):
    copies = jnp.broadcast_to(value, (size_of(axes), *value.shape))
    return lax.all_to_all(copies, axes, split_axis=0, concat_axis=0, tiled=True)


def kept(value, ranks):
    columns = jnp.arange(value.shape[-1], dtype=jnp.int32)
    return value * (columns[None, :] < ranks[:, None]).astype(value.dtype)[:, None, :]


def column_tiles(panel, col, rows, cols):
    odd = lax.rem(col, 2)
    pair = panel.shape[0] // 2

    def moved(flip):
        half = lax.bitwise_xor(odd, flip)
        part = lax.dynamic_slice_in_dim(panel, pair * half, pair, 0)
        pairs = [
            (r * cols + c, c // 2 * cols + 2 * r + (c % 2 ^ flip))
            for r in range(rows)
            for c in range(cols)
        ]
        return lax.ppermute(part, ALL, pairs)

    first, second = (moved(0), moved(1))
    low = jnp.where(odd == 0, first, second)
    high = jnp.where(odd == 0, second, first)
    return jnp.concatenate([low, high], axis=1)


def per_device(panel, inverse_factor, ranks):
    tiles, depth, width = panel.shape
    core = lax.axis_index("core")
    row = lax.axis_index(ROW)
    col = lax.axis_index(COL)
    rows, cols = (size_of(ROW), size_of(COL))
    pair = tiles * rows // cols
    part = column_tiles(panel, col, rows, cols)
    factor = lax.all_gather(inverse_factor.T, "core", axis=1, tiled=True)
    half = depth // 2
    lanes = factor.shape[1]
    factor = lax.dynamic_slice_in_dim(factor, half * core, half, 0)
    factor = sent_to_all(factor, COL)
    part_rows = part.shape[1]
    sides = width // lanes
    packed = jnp.concatenate(
        [
            factor.reshape(cols * half, lanes),
            jnp.moveaxis(part.reshape(pair, part_rows, sides, lanes), 2, 0).reshape(-1, lanes),
        ],
        axis=0,
    )
    packed = lax.all_gather(packed, ROW)
    count = cols * half
    whole = packed[:, :count].reshape(rows // 2, 2, cols, half, lanes)
    whole = whole.transpose(2, 1, 3, 0, 4).reshape(cols * depth, -1)
    mine = packed[:, count:].reshape(rows, sides, pair, part_rows, lanes)
    mine = mine.transpose(2, 0, 3, 1, 4).reshape(pair, rows * part_rows, width)
    full = sent_to_all(sent_to_all(panel, "y"), "x")
    full = full.reshape(cols, tiles, depth, width).transpose(1, 0, 2, 3)
    full = full.reshape(tiles, cols * depth, width)
    full = kept(full, lax.dynamic_slice_in_dim(ranks, row * tiles, tiles, 0))
    mine = kept(mine, lax.dynamic_slice_in_dim(ranks, col * pair, pair, 0))

    def solve(value):
        out = jnp.einsum("ba,tbr->tar", whole, value, preferred_element_type=jnp.float32)
        return out.astype(jnp.bfloat16)

    solved_full = solve(full)
    solved_mine = solve(mine)
    shares = lax.dynamic_slice_in_dim(solved_full, col * depth, depth, 1)
    core_blocks = jnp.einsum(
        "tar,uas->turs", solved_full, solved_mine, preferred_element_type=jnp.float32
    ).astype(jnp.bfloat16)
    return (shares, core_blocks)


def solution(mesh):
    split = Mesh(mesh.devices.reshape(8, 2, 4, 8), ALL)
    return jax.shard_map(
        per_device,
        mesh=split,
        in_specs=(P(ROW, COL, None), P(ROW, COL), P()),
        out_specs=(P(ROW, COL, None), P(ROW, COL, None, None)),
        check_vma=False,
    )
```

profile of v0, /device:TPU:128, one launch (start us, length us, event | category | flops | bytes accessed | tf_op | source)
XLA Modules:
  0.0 129.7 jit_solution(5983271142760320367)
XLA Ops:
  7.2 0.8 constant_dynamic-slice_fusion.1
  8.0 1.9 %collective-permute-start = (bf16[2,32,256]{2,1,0:T(8,128)(2,1)S(1)}, bf16[2,32,256]{2,1,0:T(8,128)(2,1)S(1)}, u32[]{:S(2)}, u32[]{:S(2)}) collective-permute-start(bf16[2,32,256]{2,1,0:T(8,128)(2,1)S(1)} %get-tuple-element.12), channel_id=1, source_target_pairs={{0,0},{1,1},{2,32},{3,33},{4,64},{5,65},{6,96},{7,97},{8,128},{9,1... | collective-permute-start | bytes 98312 | tf_op jit(solution)/shard_map/ppermute | solution.py:42
  9.9 6.7 %collective-permute-start.1 = (bf16[2,32,256]{2,1,0:T(8,128)(2,1)S(1)}, bf16[2,32,256]{2,1,0:T(8,128)(2,1)S(1)}, u32[]{:S(2)}, u32[]{:S(2)}) collective-permute-start(bf16[2,32,256]{2,1,0:T(8,128)(2,1)S(1)} %get-tuple-element.13), channel_id=1, source_target_pairs={{0,1},{1,0},{2,33},{3,32},{4,65},{5,64},{6,97},{7,96},{8,129},{9,1... | collective-permute-start | bytes 98312 | tf_op jit(solution)/shard_map/ppermute | solution.py:42
  16.6 3.0 %all-gather.1 = bf16[2,64,32]{1,2,0:T(8,128)(2,1)S(1)} all-gather(bf16[1,64,32]{1,2,0:T(8,128)(2,1)} %bitcast.55), channel_id=1, replica_groups=mesh['z'=8,'core'=2,'x'=4,'y'=8] {'core'}, dimensions={0}, use_global_device_ids=true | all-gather | bytes 12288 | tf_op jit(solution)/shard_map/all_gather | solution.py:58
  20.5 15.3 %all-to-all-start.2 = ((bf16[32,16,128]{2,1,0:T(8,128)(2,1)}), bf16[32,16,128]{2,1,0:T(8,128)(2,1)S(1)}, u32[]{:S(2)}, u32[]{:S(2)}) async-start(bf16[32,16,128]{2,1,0:T(8,128)(2,1)} %broadcast_in_dim.8), calls=%async_computation.2 | async-start | bytes 262144 | tf_op jit(solution)/shard_map/all_to_all | solution.py:22
  35.9 10.5 %all-to-all-done.2 = bf16[32,16,128]{2,1,0:T(8,128)(2,1)S(1)} async-done(((bf16[32,16,128]{2,1,0:T(8,128)(2,1)}), bf16[32,16,128]{2,1,0:T(8,128)(2,1)S(1)}, u32[]{:S(2)}, u32[]{:S(2)}) %all-to-all-start.2) | async-done | bytes 131104 | tf_op jit(solution)/shard_map/all_to_all | solution.py:22
  46.4 0.7 pad_maximum_fusion
  47.1 0.9 broadcast_in_dim.6
  48.0 19.4 %all_to_all.15 = bf16[8,4,32,256]{3,2,1,0:T(8,128)(2,1)S(1)} all-to-all(bf16[8,4,32,256]{3,2,1,0:T(8,128)(2,1)S(1)} %broadcast_in_dim.6), channel_id=1, replica_groups=mesh['z'=8,'core'=2,'x'=4,'y'=8] {'y'}, dimensions={0} | all-to-all | bytes 1048576 | tf_op jit(solution)/shard_map/all_to_all | solution.py:22
  67.4 1.6 %broadcast_in_dim.7 = bf16[4,8,4,32,256]{4,3,1,2,0:T(8,128)(2,1)} broadcast(bf16[8,4,32,256]{3,2,0,1:T(8,128)(2,1)S(1)} %copy.26), dimensions={1,2,3,4} | broadcast | bytes 2621440 | tf_op jit(solution)/shard_map/broadcast_in_dim | solution.py:21
  69.1 3.7 %all-to-all-start.1 = ((bf16[4,8,4,32,256]{4,3,1,2,0:T(8,128)(2,1)}), bf16[4,8,4,32,256]{4,3,1,2,0:T(8,128)(2,1)S(1)}, u32[]{:S(2)}, u32[]{:S(2)}) async-start(bf16[4,8,4,32,256]{4,3,1,2,0:T(8,128)(2,1)} %broadcast_in_dim.7), calls=%async_computation.1 | async-start | bytes 4194304 | tf_op jit(solution)/shard_map/all_to_all | solution.py:22
  73.2 23.9 %all-to-all-done.1 = bf16[4,8,4,32,256]{4,3,1,2,0:T(8,128)(2,1)S(1)} async-done(((bf16[4,8,4,32,256]{4,3,1,2,0:T(8,128)(2,1)}), bf16[4,8,4,32,256]{4,3,1,2,0:T(8,128)(2,1)S(1)}, u32[]{:S(2)}, u32[]{:S(2)}) %all-to-all-start.1) | async-done | bytes 2097184 | tf_op jit(solution)/shard_map/all_to_all | solution.py:22
  97.3 1.5 %broadcast_multiply_fusion = bf16[32,4,32,256]{3,2,0,1:T(8,128)(2,1)} fusion(bf16[32,4,32,256]{3,2,0,1:T(8,128)(2,1)S(1)} %bitcast.46, bf16[4,256]{1,0:T(4,128)(2,1)S(1)} %fusion.9), kind=kLoop, calls=%fused_computation.8 | loop fusion | flops 1048576 | bytes 4196352 | tf_op jit(solution)/shard_map/mul | solution.py:27
  98.8 1.3 slice.9
  100.1 1.8 %slice.8 = bf16[16,512,128]{2,1,0:T(8,128)(2,1)S(1)} slice(bf16[16,768,128]{2,1,0:T(8,128)(2,1)} %bitcast.50), slice={[0:16], [0:512], [0:128]} | slice | bytes 4194304 | tf_op jit(solution)/shard_map/slice | solution.py:74
  101.8 2.4 %copy.30 = bf16[32,2,16,8,128]{4,3,2,1,0:T(8,128)(2,1)S(1)} copy(bf16[32,2,16,8,128]{4,2,0,1,3:T(8,128)(2,1)S(1)} %bitcast.47) | data formatting | bytes 4194304 | tf_op jit(solution)/shard_map/transpose | solution.py:75
  104.3 2.3 %reshape.77 = bf16[1024,1024,1]{1,0,2:T(8,128)(2,1)} reshape(bf16[32,2,16,8,128]{4,3,2,1,0:T(8,128)(2,1)S(1)} %copy.30) | data formatting | bytes 4194304 | tf_op jit(solution)/shard_map/reshape | solution.py:75
  106.6 1.2 bitcast_multiply_fusion
  107.8 1.5 %mul.59 = bf16[2,1024,256]{2,1,0:T(8,128)(2,1)} reshape(bf16[2,16,64,2,128]{4,3,2,1,0:T(2,128)(2,1)S(1)} %bitcast_multiply_fusion) | data formatting | bytes 2097152 | tf_op jit(solution)/shard_map/mul | solution.py:27
  109.3 6.1 %convolution_convert_fusion = bf16[4,256,1024]{2,1,0:T(8,128)(2,1)} fusion(bf16[4,1024,256]{2,1,0:T(8,128)(2,1)} %bitcast.51, bf16[1024,1024,1]{1,0,2:T(8,128)(2,1)} %reshape.77), kind=kOutput, calls=%fused_computation.2 | convolution fusion | flops 2148532224 | bytes 6291456 | tf_op jit(solution)/shard_map/ba,tbr->tar/dot_general | solution.py:85
  115.4 4.3 %fusion.6 = bf16[4,2,256,256]{2,3,0,1:T(8,128)(2,1)S(1)} fusion(bf16[4,256,1024]{2,1,0:T(8,128)(2,1)} %convolution_convert_fusion, bf16[2,1024,256]{2,1,0:T(8,128)(2,1)} %mul.59, bf16[1024,1024,1]{1,0,2:T(8,128)(2,1)S(1)} %copy-done), kind=kOutput, calls=%fused_computation.6 | convolution fusion | flops 2148532224 | bytes 6291456 | tf_op jit(solution)/shard_map/tar,uas->turs/dot_general | solution.py:91
  119.7 1.1 dynamic-slice_bitcast_fusion
  120.8 0.8 copy.35
  121.6 1.3 %copy.36 = bf16[4,2,256,256]{3,2,1,0:T(8,128)(2,1)} copy(bf16[4,2,256,256]{2,3,0,1:T(8,128)(2,1)S(1)} %fusion.6) | data formatting | bytes 2097152
  (24 shorter events, 1.4 us)
Async XLA Ops:
  8.0 27.9 %collective-permute-start = (bf16[2,32,256]{2,1,0:T(8,128)(2,1)S(1)}, bf16[2,32,256]{2,1,0:T(8,128)(2,1)S(1)}, u32[]{:S(2)}, u32[]{:S(2)}) collective-permute-start(bf16[2,32,256]{2,1,0:T(8,128)(2,1)S(1)} %get-tuple-element.12), channel_id=1, source_target_pairs={{0,0},{1,1},{2,32},{3,33},{4,64},{5,65},{6,96},{7,97},{8,128},{9,1... | collective-permute-start | bytes 98312 | tf_op jit(solution)/shard_map/ppermute | solution.py:42
  9.9 25.9 %collective-permute-start.1 = (bf16[2,32,256]{2,1,0:T(8,128)(2,1)S(1)}, bf16[2,32,256]{2,1,0:T(8,128)(2,1)S(1)}, u32[]{:S(2)}, u32[]{:S(2)}) collective-permute-start(bf16[2,32,256]{2,1,0:T(8,128)(2,1)S(1)} %get-tuple-element.13), channel_id=1, source_target_pairs={{0,1},{1,0},{2,33},{3,32},{4,65},{5,64},{6,97},{7,96},{8,129},{9,1... | collective-permute-start | bytes 98312 | tf_op jit(solution)/shard_map/ppermute | solution.py:42
  20.5 25.9 %all-to-all-start.2 = ((bf16[32,16,128]{2,1,0:T(8,128)(2,1)}), bf16[32,16,128]{2,1,0:T(8,128)(2,1)S(1)}, u32[]{:S(2)}, u32[]{:S(2)}) async-start(bf16[32,16,128]{2,1,0:T(8,128)(2,1)} %broadcast_in_dim.8), calls=%async_computation.2 | async-start | bytes 262144 | tf_op jit(solution)/shard_map/all_to_all | solution.py:22
  35.8 63.0 %all-gather.4.cloned.1.call-start = ((), (), s32[]{:S(2)}) async-start(), calls=%async_computation.3 | async-start | bytes 3342336 | tf_op jit(solution)/shard_map/all_gather | solution.py:72
  69.1 3.8 %copy-start.1 = (s32[64]{0:T(128)S(1)}, s32[64]{0:T(128)}, u32[]{:S(2)}) copy-start(s32[64]{0:T(128)} %param.5) | copy-start | bytes 772
  69.1 28.0 %all-to-all-start.1 = ((bf16[4,8,4,32,256]{4,3,1,2,0:T(8,128)(2,1)}), bf16[4,8,4,32,256]{4,3,1,2,0:T(8,128)(2,1)S(1)}, u32[]{:S(2)}, u32[]{:S(2)}) async-start(bf16[4,8,4,32,256]{4,3,1,2,0:T(8,128)(2,1)} %broadcast_in_dim.7), calls=%async_computation.1 | async-start | bytes 4194304 | tf_op jit(solution)/shard_map/all_to_all | solution.py:22
  109.3 6.1 %copy-start = (bf16[1024,1024,1]{1,0,2:T(8,128)(2,1)S(1)}, bf16[1024,1024,1]{1,0,2:T(8,128)(2,1)}, u32[]{:S(2)}) copy-start(bf16[1024,1024,1]{1,0,2:T(8,128)(2,1)} %reshape.77) | copy-start | bytes 6291460
Sparse Core Ops, SparseCore 0:
  47.2 37.9 all-gather.3
where the time goes:
time: 130 us
  waiting for transfers between devices  34.4 us (26%)
  starting transfers between devices  27.7 us (21%)
  blocking collectives  22.4 us (17%)
  local copies, waits for them, and re-layouts  16.9 us (13%)
  between operations  14.2 us (11%)
  matrix products  10.4 us (8%)
  other arithmetic  3.59 us (3%)
    all_to_all x2, waiting for transfers between devices, sent_to_all(): return lax.all_to_all(copies, axes, split_axis=0, concat_axis=0, tiled=True)  34.4 us
    all_to_all x1, blocking collectives, sent_to_all(): return lax.all_to_all(copies, axes, split_axis=0, concat_axis=0, tiled=True)  19.4 us
    all_to_all x2, starting transfers between devices, sent_to_all(): return lax.all_to_all(copies, axes, split_axis=0, concat_axis=0, tiled=True)  19 us
    ppermute x2, starting transfers between devices, moved(): return lax.ppermute(part, ALL, pairs)  8.64 us
    dot_general x1, matrix products, solve(): jnp.einsum('ba,tbr->tar', whole, value, preferred_element_type=jnp.float32)  6.11 us
    dot_general x1, matrix products, per_device(): jnp.einsum('tar,uas->turs', solved_full, solved_mine, preferred_element_t...  4.27 us
    broadcast_in_dim x3, local copies, waits for them, and re-layouts, sent_to_all(): copies = jnp.broadcast_to(value, (size_of(axes), *value.shape))  3.21 us
    all_gather x1, blocking collectives, per_device(): factor = lax.all_gather(inverse_factor.T, 'core', axis=1, tiled=True)  3.04 us
  transfers between devices with their start and end apart: 5, of which 2 were waited for; matrix products, arithmetic and copies ran while one was open for 4% of the time, Pallas kernels for 0%

commit v1 on v0

--- a/solution.py
+++ b/solution.py
@@ -55,7 +55,9 @@
     rows, cols = (size_of(ROW), size_of(COL))
     pair = tiles * rows // cols
     part = column_tiles(panel, col, rows, cols)
-    factor = lax.all_gather(inverse_factor.T, "core", axis=1, tiled=True)
+    factor = jnp.concatenate(
+        lax.all_to_all(jnp.stack([inverse_factor.T] * lax.axis_size("core")), "core", 0, 0), axis=1
+    )
     half = depth // 2
     lanes = factor.shape[1]
     factor = lax.dynamic_slice_in_dim(factor, half * core, half, 0)

time: 130 us -> 135 us (1.038)
  the two profiles are of different devices: /device:TPU:128 before, /device:TPU:64 now
where the time goes in v1:
time: 135 us; the launch traced here: 134 us
  waiting for transfers between devices  36.6 us (27%)
  starting transfers between devices  29.2 us (22%)
  blocking collectives  21.7 us (16%)
  local copies, waits for them, and re-layouts  17.7 us (13%)
  between operations  14.2 us (11%)
  matrix products  10.4 us (8%)
  other arithmetic  4.38 us (3%)
    all_to_all x2, waiting for transfers between devices, sent_to_all(): return lax.all_to_all(copies, axes, split_axis=0, concat_axis=0, tiled=True)  36.6 us
    all_to_all x1, blocking collectives, sent_to_all(): return lax.all_to_all(copies, axes, split_axis=0, concat_axis=0, tiled=True)  21.7 us
    all_to_all x2, starting transfers between devices, sent_to_all(): return lax.all_to_all(copies, axes, split_axis=0, concat_axis=0, tiled=True)  15.2 us
    ppermute x2, starting transfers between devices, moved(): return lax.ppermute(part, ALL, pairs)  10.8 us
    dot_general x1, matrix products, solve(): jnp.einsum('ba,tbr->tar', whole, value, preferred_element_type=jnp.float32)  6.12 us
    dot_general x1, matrix products, per_device(): jnp.einsum('tar,uas->turs', solved_full, solved_mine, preferred_element_t...  4.27 us
    all_to_all x1, starting transfers between devices, per_device(): lax.all_to_all(jnp.stack([inverse_factor.T] * lax.axis_size('core')), 'co...  3.23 us
    broadcast_in_dim x3, local copies, waits for them, and re-layouts, sent_to_all(): copies = jnp.broadcast_to(value, (size_of(axes), *value.shape))  3.21 us
  transfers between devices with their start and end apart: 6, of which 2 were waited for; matrix products, arithmetic and copies ran while one was open for 5% of the time, Pallas kernels for 0%

profile of v1, /device:TPU:64, one launch (start us, length us, event | category | flops | bytes accessed | tf_op | source)
XLA Modules:
  0.0 134.2 jit_solution(3589659635594121485)
XLA Ops:
  7.2 0.8 pad_maximum_fusion.2
  8.6 3.2 %all-to-all-start.2 = ((bf16[2,2,1024]{2,1,0:T(2,128)(2,1)}), bf16[2,2,1024]{2,1,0:T(2,128)(2,1)S(1)}, u32[]{:S(2)}, u32[]{:S(2)}) async-start(bf16[2,2,1024]{2,1,0:T(2,128)(2,1)} %reshape.87), calls=%async_computation.2 | async-start | bytes 16384 | tf_op jit(solution)/shard_map/all_to_all | solution.py:59
  11.9 0.8 constant_dynamic-slice_fusion.1
  12.7 6.8 %collective-permute-start = (bf16[2,32,256]{2,1,0:T(8,128)(2,1)S(1)}, bf16[2,32,256]{2,1,0:T(8,128)(2,1)S(1)}, u32[]{:S(2)}, u32[]{:S(2)}) collective-permute-start(bf16[2,32,256]{2,1,0:T(8,128)(2,1)S(1)} %get-tuple-element.12), channel_id=1, source_target_pairs={{0,0},{1,1},{2,32},{3,33},{4,64},{5,65},{6,96},{7,97},{8,128},{9,1... | collective-permute-start | bytes 98312 | tf_op jit(solution)/shard_map/ppermute | solution.py:42
  19.5 3.9 %collective-permute-start.1 = (bf16[2,32,256]{2,1,0:T(8,128)(2,1)S(1)}, bf16[2,32,256]{2,1,0:T(8,128)(2,1)S(1)}, u32[]{:S(2)}, u32[]{:S(2)}) collective-permute-start(bf16[2,32,256]{2,1,0:T(8,128)(2,1)S(1)} %get-tuple-element.13), channel_id=1, source_target_pairs={{0,1},{1,0},{2,33},{3,32},{4,65},{5,64},{6,97},{7,96},{8,129},{9,1... | collective-permute-start | bytes 98312 | tf_op jit(solution)/shard_map/ppermute | solution.py:42
  24.3 11.5 %all-to-all-start.3 = ((bf16[32,16,128]{2,1,0:T(8,128)(2,1)}), bf16[32,16,128]{2,1,0:T(8,128)(2,1)S(1)}, u32[]{:S(2)}, u32[]{:S(2)}) async-start(bf16[32,16,128]{2,1,0:T(8,128)(2,1)} %broadcast_in_dim.8), calls=%async_computation.3 | async-start | bytes 262144 | tf_op jit(solution)/shard_map/all_to_all | solution.py:22
  35.9 10.2 %all-to-all-done.3 = bf16[32,16,128]{2,1,0:T(8,128)(2,1)S(1)} async-done(((bf16[32,16,128]{2,1,0:T(8,128)(2,1)}), bf16[32,16,128]{2,1,0:T(8,128)(2,1)S(1)}, u32[]{:S(2)}, u32[]{:S(2)}) %all-to-all-start.3) | async-done | bytes 131104 | tf_op jit(solution)/shard_map/all_to_all | solution.py:22
  46.8 0.9 broadcast_in_dim.6
  47.7 21.7 %all_to_all.20 = bf16[8,4,32,256]{3,2,1,0:T(8,128)(2,1)S(1)} all-to-all(bf16[8,4,32,256]{3,2,1,0:T(8,128)(2,1)S(1)} %broadcast_in_dim.6), channel_id=1, replica_groups=mesh['z'=8,'core'=2,'x'=4,'y'=8] {'y'}, dimensions={0} | all-to-all | bytes 1048576 | tf_op jit(solution)/shard_map/all_to_all | solution.py:22
  69.4 1.6 %broadcast_in_dim.7 = bf16[4,8,4,32,256]{4,3,1,2,0:T(8,128)(2,1)} broadcast(bf16[8,4,32,256]{3,2,0,1:T(8,128)(2,1)S(1)} %copy.25), dimensions={1,2,3,4} | broadcast | bytes 2621440 | tf_op jit(solution)/shard_map/broadcast_in_dim | solution.py:21
  71.1 3.7 %all-to-all-start.1 = ((bf16[4,8,4,32,256]{4,3,1,2,0:T(8,128)(2,1)}), bf16[4,8,4,32,256]{4,3,1,2,0:T(8,128)(2,1)S(1)}, u32[]{:S(2)}, u32[]{:S(2)}) async-start(bf16[4,8,4,32,256]{4,3,1,2,0:T(8,128)(2,1)} %broadcast_in_dim.7), calls=%async_computation.1 | async-start | bytes 4194304 | tf_op jit(solution)/shard_map/all_to_all | solution.py:22
  75.2 26.5 %all-to-all-done.1 = bf16[4,8,4,32,256]{4,3,1,2,0:T(8,128)(2,1)S(1)} async-done(((bf16[4,8,4,32,256]{4,3,1,2,0:T(8,128)(2,1)}), bf16[4,8,4,32,256]{4,3,1,2,0:T(8,128)(2,1)S(1)}, u32[]{:S(2)}, u32[]{:S(2)}) %all-to-all-start.1) | async-done | bytes 2097184 | tf_op jit(solution)/shard_map/all_to_all | solution.py:22
  101.8 1.5 %broadcast_multiply_fusion = bf16[32,4,32,256]{3,2,0,1:T(8,128)(2,1)} fusion(bf16[32,4,32,256]{3,2,0,1:T(8,128)(2,1)S(1)} %bitcast.45, bf16[4,256]{1,0:T(4,128)(2,1)S(1)} %fusion.9), kind=kLoop, calls=%fused_computation.8 | loop fusion | flops 1048576 | bytes 4196352 | tf_op jit(solution)/shard_map/mul | solution.py:27
  103.3 1.3 slice.9
  104.6 1.8 %slice.8 = bf16[16,512,128]{2,1,0:T(8,128)(2,1)S(1)} slice(bf16[16,768,128]{2,1,0:T(8,128)(2,1)} %bitcast.49), slice={[0:16], [0:512], [0:128]} | slice | bytes 4194304 | tf_op jit(solution)/shard_map/slice | solution.py:76
  106.4 2.4 %copy.29 = bf16[32,2,16,8,128]{4,3,2,1,0:T(8,128)(2,1)S(1)} copy(bf16[32,2,16,8,128]{4,2,0,1,3:T(8,128)(2,1)S(1)} %bitcast.46) | data formatting | bytes 4194304 | tf_op jit(solution)/shard_map/transpose | solution.py:77
  108.8 2.3 %reshape.83 = bf16[1024,1024,1]{1,0,2:T(8,128)(2,1)} reshape(bf16[32,2,16,8,128]{4,3,2,1,0:T(8,128)(2,1)S(1)} %copy.29) | data formatting | bytes 4194304 | tf_op jit(solution)/shard_map/reshape | solution.py:77
  111.1 1.2 bitcast_multiply_fusion
  112.4 1.5 %mul.59 = bf16[2,1024,256]{2,1,0:T(8,128)(2,1)} reshape(bf16[2,16,64,2,128]{4,3,2,1,0:T(2,128)(2,1)S(1)} %bitcast_multiply_fusion) | data formatting | bytes 2097152 | tf_op jit(solution)/shard_map/mul | solution.py:27
  113.8 6.1 %convolution_convert_fusion = bf16[4,256,1024]{2,1,0:T(8,128)(2,1)} fusion(bf16[4,1024,256]{2,1,0:T(8,128)(2,1)} %bitcast.50, bf16[1024,1024,1]{1,0,2:T(8,128)(2,1)} %reshape.83), kind=kOutput, calls=%fused_computation.2 | convolution fusion | flops 2148532224 | bytes 6291456 | tf_op jit(solution)/shard_map/ba,tbr->tar/dot_general | solution.py:87
  120.0 4.3 %fusion.6 = bf16[4,2,256,256]{2,3,0,1:T(8,128)(2,1)S(1)} fusion(bf16[4,256,1024]{2,1,0:T(8,128)(2,1)} %convolution_convert_fusion, bf16[2,1024,256]{2,1,0:T(8,128)(2,1)} %mul.59, bf16[1024,1024,1]{1,0,2:T(8,128)(2,1)S(1)} %copy-done), kind=kOutput, calls=%fused_computation.6 | convolution fusion | flops 2148532224 | bytes 6291456 | tf_op jit(solution)/shard_map/tar,uas->turs/dot_general | solution.py:93
  124.2 1.1 dynamic-slice_bitcast_fusion
  125.3 0.8 copy.34
  126.1 1.3 copy.35
  (28 shorter events, 2.9 us)
Async XLA Ops:
  8.6 14.8 %all-to-all-start.2 = ((bf16[2,2,1024]{2,1,0:T(2,128)(2,1)}), bf16[2,2,1024]{2,1,0:T(2,128)(2,1)S(1)}, u32[]{:S(2)}, u32[]{:S(2)}) async-start(bf16[2,2,1024]{2,1,0:T(2,128)(2,1)} %reshape.87), calls=%async_computation.2 | async-start | bytes 16384 | tf_op jit(solution)/shard_map/all_to_all | solution.py:59
  12.7 23.2 %collective-permute-start = (bf16[2,32,256]{2,1,0:T(8,128)(2,1)S(1)}, bf16[2,32,256]{2,1,0:T(8,128)(2,1)S(1)}, u32[]{:S(2)}, u32[]{:S(2)}) collective-permute-start(bf16[2,32,256]{2,1,0:T(8,128)(2,1)S(1)} %get-tuple-element.12), channel_id=1, source_target_pairs={{0,0},{1,1},{2,32},{3,33},{4,64},{5,65},{6,96},{7,97},{8,128},{9,1... | collective-permute-start | bytes 98312 | tf_op jit(solution)/shard_map/ppermute | solution.py:42
  19.5 16.4 %collective-permute-start.1 = (bf16[2,32,256]{2,1,0:T(8,128)(2,1)S(1)}, bf16[2,32,256]{2,1,0:T(8,128)(2,1)S(1)}, u32[]{:S(2)}, u32[]{:S(2)}) collective-permute-start(bf16[2,32,256]{2,1,0:T(8,128)(2,1)S(1)} %get-tuple-element.13), channel_id=1, source_target_pairs={{0,1},{1,0},{2,33},{3,32},{4,65},{5,64},{6,97},{7,96},{8,129},{9,1... | collective-permute-start | bytes 98312 | tf_op jit(solution)/shard_map/ppermute | solution.py:42
  24.3 21.8 %all-to-all-start.3 = ((bf16[32,16,128]{2,1,0:T(8,128)(2,1)}), bf16[32,16,128]{2,1,0:T(8,128)(2,1)S(1)}, u32[]{:S(2)}, u32[]{:S(2)}) async-start(bf16[32,16,128]{2,1,0:T(8,128)(2,1)} %broadcast_in_dim.8), calls=%async_computation.3 | async-start | bytes 262144 | tf_op jit(solution)/shard_map/all_to_all | solution.py:22
  35.8 67.5 %all-gather.3.cloned.1.call-start = ((), (), s32[]{:S(2)}) async-start(), calls=%async_computation.4 | async-start | bytes 3342336 | tf_op jit(solution)/shard_map/all_gather | solution.py:74
  71.1 3.8 %copy-start.1 = (s32[64]{0:T(128)S(1)}, s32[64]{0:T(128)}, u32[]{:S(2)}) copy-start(s32[64]{0:T(128)} %param.5) | copy-start | bytes 772
  71.1 30.5 %all-to-all-start.1 = ((bf16[4,8,4,32,256]{4,3,1,2,0:T(8,128)(2,1)}), bf16[4,8,4,32,256]{4,3,1,2,0:T(8,128)(2,1)S(1)}, u32[]{:S(2)}, u32[]{:S(2)}) async-start(bf16[4,8,4,32,256]{4,3,1,2,0:T(8,128)(2,1)} %broadcast_in_dim.7), calls=%async_computation.1 | async-start | bytes 4194304 | tf_op jit(solution)/shard_map/all_to_all | solution.py:22
  113.8 6.1 %copy-start = (bf16[1024,1024,1]{1,0,2:T(8,128)(2,1)S(1)}, bf16[1024,1024,1]{1,0,2:T(8,128)(2,1)}, u32[]{:S(2)}) copy-start(bf16[1024,1024,1]{1,0,2:T(8,128)(2,1)} %reshape.83) | copy-start | bytes 6291460
Sparse Core Ops, SparseCore 0:
  46.9 42.6 all-gather.2
